TPU v7x, 512 devices: a whole 4x8x8 slice. The times are simulated.
512 devices in a mesh: seq: 64 (over y, z), trk: 8 (over x, core).
Axes of the slice: x: 4, y: 8, z: 8, core: 2. Of those that a mesh axis runs over, the one named last changes fastest.
Arguments:
- embeddings: bfloat16 [4, 8192, 1920], P(None, 'seq', 'trk'), may hold values from -16 to 16
- head: bfloat16 [1920, 4096], P(None, 'trk'), may hold values from -0.125 to 0.125
- exon_starts: int32 [4, 128, 8], replicated, may hold values from 0 to 8184, as said below
- exon_lengths: int32 [4, 128, 8], replicated, may hold values from 1 to 8, as said below
- gene_owner: int32 [4, 128], replicated, may hold values from 0 to 63, as said below
- gene_targets: float32 [4, 256, 4096], P(None, 'seq', 'trk'), may hold values from 2 to 400, as said below
Outputs:
- gene_pred: float32 [4, 256, 4096], P(None, 'seq', 'trk')
- loss: float32 [4, 4096], P(None, 'trk')
- grad_head: float32 [1920, 4096], P('seq', 'trk')
Inputs may be any that keep to these rules, and one draw needn't show every extreme that they name: `exon_starts`: each gene has 8 exon blocks; blocks may intersect. Some block of each window starts at 0 and some at 8184. `exon_lengths`: some block of each window has length 8. `gene_owner`: in each window no owner holds more than 4 genes, and some owner holds exactly 4. `gene_targets`: entries of empty slots are read by nothing.
All inputs are finite; a program needn't handle non-finite values.
Results may differ from a plain program's by a relative error of at most 0.0041.
Values may be sent and summed in bfloat16 or wider, within the bound.
No kernel may reach another device: no remote copies, remote signals or barrier semaphores. Data moves between devices by JAX's collectives and lax.ppermute only.
A program may use at most 64 MiB of HBM per device.

v0:
```python
import jax
import jax.numpy as jnp
from jax import lax
from jax.sharding import PartitionSpec as P


def slot_table(gene_owner, capacity):
    genes = gene_owner.shape[1]
    same = gene_owner[:, :, None] == gene_owner[:, None, :]
    earlier = jnp.arange(genes)[None, :] < jnp.arange(genes)[:, None]
    ahead = jnp.sum((same & earlier[None]).astype(jnp.int32), axis=2)
    return gene_owner * capacity + ahead


def coverage(starts, lengths, positions):
    where_bin = positions[None, None, None, :]
    inside = (where_bin >= starts[..., None]) & (where_bin < (starts + lengths)[..., None])
    return jnp.sum(inside.astype(jnp.float32), axis=2)


def fold_sources(received):
    return jnp.sum(received, axis=1)


def per_device(embeddings, head, exon_starts, exon_lengths, gene_owner, gene_targets):
    seq_devices = lax.axis_size("seq")
    seq_place = lax.axis_index("seq")
    windows, bin_dev, _ = embeddings.shape
    genes = gene_owner.shape[1]
    capacity = gene_targets.shape[1]
    slot_total = seq_devices * capacity
    whole = lax.all_gather(embeddings, "trk", axis=2, tiled=True)
    logits = jnp.einsum("wbd,dt->wbt", whole, head, preferred_element_type=jnp.float32)
    pred = jax.nn.softplus(logits).astype(jnp.bfloat16)
    positions = seq_place * bin_dev + jnp.arange(bin_dev, dtype=jnp.int32)
    cover = coverage(exon_starts, exon_lengths, positions)
    slot_of = slot_table(gene_owner, capacity)
    onehot = (slot_of[..., None] == jnp.arange(slot_total, dtype=jnp.int32)).astype(jnp.float32)
    member = jnp.einsum("wgs,wgb->wsb", onehot, cover, precision=lax.Precision.HIGHEST).astype(
        jnp.bfloat16
    )
    valid = jnp.sum(onehot, axis=1)
    valid_here = lax.dynamic_slice_in_dim(valid, seq_place * capacity, capacity, 1)
    targets_here = gene_targets * valid_here[..., None]
    target_part = jnp.sum(targets_here, axis=1)
    partial_value = jnp.einsum("wsb,wbt->wst", member, pred, preferred_element_type=jnp.float32)
    blocks = partial_value.reshape(windows, seq_devices, capacity, partial_value.shape[2])
    gene_here = fold_sources(lax.all_to_all(blocks, "seq", split_axis=1, concat_axis=1, tiled=True))
    safe = jnp.where(valid_here[..., None] > 0, gene_here, 1.0)
    fit_part = jnp.sum(targets_here * jnp.log(safe), axis=1)
    total, target_sum, fit = lax.psum((jnp.sum(gene_here, axis=1), target_part, fit_part), "seq")
    scale_rows = (genes / target_sum)[:, None, :]
    gene_grad = (
        scale_rows
        * (
            valid_here[..., None] * (0.2 + 0.8 * target_sum / total)[:, None, :]
            - targets_here / safe
        )
    ).astype(jnp.bfloat16)
    bin_grad = jnp.einsum(
        "wsb,wst->wbt",
        member,
        lax.all_gather(gene_grad, "seq", axis=1, tiled=True),
        preferred_element_type=jnp.float32,
    )
    logit_grad = (bin_grad * jax.nn.sigmoid(logits)).astype(jnp.bfloat16)
    grad_head = lax.psum_scatter(
        jnp.einsum("wbd,wbt->dt", whole, logit_grad, preferred_element_type=jnp.float32),
        "seq",
        scatter_dimension=0,
        tiled=True,
    )
    log_total = jnp.log(total)
    loss = (-fit + target_sum * log_total + 0.2 * (total - target_sum * log_total)) / target_sum
    return (gene_here, loss, grad_head)


def solution(mesh):
    return jax.shard_map(
        per_device,
        mesh=mesh,
        in_specs=(P(None, "seq", "trk"), P(None, "trk"), P(), P(), P(), P(None, "seq", "trk")),
        out_specs=(P(None, "seq", "trk"), P(None, "trk"), P("seq", "trk")),
        check_vma=False,
    )
```

profile of v0, /device:TPU:2, one launch (start us, length us, event | category | flops | bytes accessed | tf_op | source)
XLA Modules:
  0.0 664.6 jit_solution(17121487797619391338)
XLA Ops:
  7.2 0.0 all-gather.3.cloned.1.call-start
  7.2 0.7 all-gather.3.cloned.1.call-update
  7.9 0.8 copy.28
  8.8 0.7 add.46
  9.5 0.1 copy.29
  9.7 1.0 convert_reduce_fusion.2
  10.7 0.7 multiply_add_fusion
  11.4 1.4 convert_reduce_fusion
  12.8 0.4 convolution_convert_fusion
  13.2 30.7 %all-gather.3.cloned.1.call-done = bf16[4,128,1920]{1,2,0:T(8,128)(2,1)} async-done(((bf16[4,128,240]{1,2,0:T(8,128)(2,1)}), bf16[4,128,1920]{1,2,0:T(8,128)(2,1)}) %all-gather.3.cloned.1.call-update) | async-done | bytes 1966096 | tf_op jit(solution)/shard_map/all_gather | solution.py:32
  43.9 2.8 fusion.13
  46.8 2.2 fusion.9
  48.9 2.9 reshape.35
  51.8 3.5 copy.30
  55.4 13.6 %all-to-all-start = ((f32[4,64,4,512]{3,2,0,1:T(4,128)}), f32[4,64,4,512]{3,2,0,1:T(4,128)}, u32[]{:S(2)}, u32[]{:S(2)}) async-start(f32[4,64,4,512]{3,2,0,1:T(4,128)} %copy.30), calls=%async_computation | async-start | bytes 4194304 | tf_op jit(solution)/shard_map/all_to_all | solution.py:48
  68.9 0.0 all-gather.5.cloned.1.call-start
  69.0 0.1 convert_reduce_fusion.1
  69.1 0.1 broadcast_compare_fusion
  69.2 51.5 %all-to-all-done = f32[4,64,4,512]{3,2,0,1:T(4,128)} async-done(((f32[4,64,4,512]{3,2,0,1:T(4,128)}), f32[4,64,4,512]{3,2,0,1:T(4,128)}, u32[]{:S(2)}, u32[]{:S(2)}) %all-to-all-start) | async-done | bytes 2097184 | tf_op jit(solution)/shard_map/all_to_all | solution.py:48
  120.7 2.1 fusion.20
  122.8 0.1 multiply_reduce_fusion
  122.9 282.3 %all-reduce.1 = (f32[4,512]{1,0:T(4,128)S(1)}, f32[4,512]{1,0:T(4,128)S(1)}, f32[4,512]{1,0:T(4,128)S(1)}) all-reduce(f32[4,512]{1,0:T(4,128)S(1)} %get-tuple-element.18, f32[4,512]{1,0:T(4,128)S(1)} %get-tuple-element.15, f32[4,512]{1,0:T(4,128)S(1)} %get-tuple-element.17), channel_id=1, replica_groups=mesh['seq'=64,'trk'=8] {'seq'}, use_global_device_ids=true, to_apply=%region_7.8 | all-reduce | flops 6144 | bytes 49152 | tf_op jit(solution)/shard_map/psum | solution.py:51
  405.2 0.6 fusion.16
  405.8 0.1 multiply_convert_fusion
  405.9 0.6 copy.31
  406.5 0.0 all-reduce.4.cloned.1.call-start
  406.6 76.9 %all-gather.5.cloned.1.call-done = bf16[4,256,512]{2,0,1:T(4,128)(2,1)} async-done(((bf16[4,4,512]{2,0,1:T(4,128)(2,1)}), bf16[4,256,512]{2,0,1:T(4,128)(2,1)}) %all-gather.5.cloned.1.call-update) | async-done | bytes 1048592 | tf_op jit(solution)/shard_map/all_gather | solution.py:63
  483.5 5.5 convolution_bitcast_fusion
  489.0 1.3 dynamic-slice
  490.9 165.2 %all-reduce.4.cloned.1.call-done = f32[1920,512]{0,1:T(8,128)} async-done(((f32[1920,512]{0,1:T(8,128)}), f32[1920,512]{0,1:T(8,128)}) %all-reduce.4.cloned.1.call-update) | async-done | bytes 3932176
  656.1 1.2 constant_dynamic-slice_fusion
  657.3 0.8 copy.35
  (10 shorter events, 0.1 us)
Async XLA Ops:
  7.2 36.7 %copy-start = (bf16[1920,512]{1,0:T(8,128)(2,1)S(1)}, bf16[1920,512]{1,0:T(8,128)(2,1)}, u32[]{:S(2)}) copy-start(bf16[1920,512]{1,0:T(8,128)(2,1)} %param.7) | copy-start | bytes 5898244
  7.2 36.7 %all-gather.3.cloned.1.call-start = ((), (), s32[]{:S(2)}) async-start(), calls=%async_computation.1 | async-start | bytes 2211840 | tf_op jit(solution)/shard_map/all_gather | solution.py:32
  55.4 65.3 %all-to-all-start = ((f32[4,64,4,512]{3,2,0,1:T(4,128)}), f32[4,64,4,512]{3,2,0,1:T(4,128)}, u32[]{:S(2)}, u32[]{:S(2)}) async-start(f32[4,64,4,512]{3,2,0,1:T(4,128)} %copy.30), calls=%async_computation | async-start | bytes 4194304 | tf_op jit(solution)/shard_map/all_to_all | solution.py:48
  68.9 53.8 %copy-start.2 = (f32[4,4,512]{2,1,0:T(4,128)S(1)}, f32[4,4,512]{2,1,0:T(4,128)}, u32[]{:S(2)}) copy-start(f32[4,4,512]{2,1,0:T(4,128)} %param.11) | copy-start | bytes 98308
  68.9 414.6 %all-gather.5.cloned.1.call-start = ((), (), s32[]{:S(2)}) async-start(), calls=%async_computation.2 | async-start | bytes 1064960 | tf_op jit(solution)/shard_map/all_gather | solution.py:63
  122.7 366.2 %copy-start.1 = (f32[4,4,512]{2,1,0:T(4,128)}, f32[4,4,512]{2,1,0:T(4,128)S(1)}, u32[]{:S(2)}) copy-start(f32[4,4,512]{2,1,0:T(4,128)S(1)} %get-tuple-element.16) | copy-start | bytes 98308
  406.5 249.6 %all-reduce.4.cloned.1.call-start = ((), (), s32[]{:S(2)}) async-start(), calls=%async_computation.3 | async-start | bytes 7864320
Sparse Core Ops, SparseCore 0:
  10.1 33.7 all-gather.2
  406.7 76.7 all-gather.4
  489.1 166.9 all-reduce.3
where the time goes:
time: 665 us
  waiting for transfers between devices  325 us (49%)
  blocking collectives  282 us (42%)
  between operations  14.5 us (2%)
  starting transfers between devices  13.7 us (2%)
  local copies, waits for them, and re-layouts  11.2 us (2%)
  matrix products  10.9 us (2%)
  other arithmetic  7 us (1%)
    psum x1, blocking collectives, per_device(): lax.psum((jnp.sum(gene_here, axis=1), target_part, fit_part), 'seq')  282 us
    unnamed x4, waiting for transfers between devices  166 us
    all_gather x1, waiting for transfers between devices, per_device(): lax.all_gather(gene_grad, 'seq', axis=1, tiled=True)  76.9 us
    all_to_all x1, waiting for transfers between devices, per_device(): lax.all_to_all(blocks, 'seq', split_axis=1, concat_axis=1, tiled=True)  51.5 us
    all_gather x1, waiting for transfers between devices, per_device(): whole = lax.all_gather(embeddings, 'trk', axis=2, tiled=True)  30.7 us
    all_to_all x1, starting transfers between devices, per_device(): lax.all_to_all(blocks, 'seq', split_axis=1, concat_axis=1, tiled=True)  13.6 us
  transfers between devices with their start and end apart: 4, of which 4 were waited for; matrix products, arithmetic and copies ran while one was open for 1% of the time, Pallas kernels for 0%

commit v1 on v0

--- a/solution.py
+++ b/solution.py
@@ -1,7 +1,19 @@
+import functools
 import jax
 import jax.numpy as jnp
 from jax import lax
 from jax.sharding import PartitionSpec as P
+
+
+def _extend_rates(t0, pos_dim):
+    even = jnp.concatenate(
+        lax.all_to_all(jnp.stack([t0 for _ in range(lax.axis_size("seq"))]), "seq", 0, 0),
+        axis=pos_dim,
+    )
+    return even
+
+
+_find_run = functools.partial(_extend_rates, pos_dim=1)
 
 
 def slot_table(gene_owner, capacity):
@@ -58,10 +70,7 @@
         )
     ).astype(jnp.bfloat16)
     bin_grad = jnp.einsum(
-        "wsb,wst->wbt",
-        member,
-        lax.all_gather(gene_grad, "seq", axis=1, tiled=True),
-        preferred_element_type=jnp.float32,
+        "wsb,wst->wbt", member, _find_run(gene_grad), preferred_element_type=jnp.float32
     )
     logit_grad = (bin_grad * jax.nn.sigmoid(logits)).astype(jnp.bfloat16)
     grad_head = lax.psum_scatter(

time: 665 us -> 615 us (0.925)
  waiting for transfers between devices: 325 us -> 246 us
  blocking collectives: 282 us -> 311 us
    all_gather x1 -> x0, waiting for transfers between devices: 76.9 us -> none  [per_device(): lax.all_gather(gene_grad, 'seq', axis=1, tiled=True)]
    all_to_all x0 -> x1, blocking collectives: none -> 26.6 us  [_extend_rates(): lax.all_to_all(jnp.stack([t0 for _ in range(lax.axis_size('seq'))]), 'seq...]
    unnamed x4 -> x3, waiting for transfers between devices: 166 us -> 164 us
  transfers between devices with their start and end apart: 4 -> 3, of which waited for: 4 -> 3; matrix products, arithmetic and copies ran while one was open for 1% -> 1% of each run, Pallas kernels for 0% -> 0%
where the time goes in v1:
time: 615 us
  blocking collectives  311 us (51%)
  waiting for transfers between devices  246 us (40%)
  between operations  14.8 us (2%)
  starting transfers between devices  13.6 us (2%)
  local copies, waits for them, and re-layouts  11.1 us (2%)
  matrix products  10.9 us (2%)
  other arithmetic  7 us (1%)
    psum x1, blocking collectives, per_device(): lax.psum((jnp.sum(gene_here, axis=1), target_part, fit_part), 'seq')  285 us
    unnamed x3, waiting for transfers between devices  164 us
    all_to_all x1, waiting for transfers between devices, per_device(): lax.all_to_all(blocks, 'seq', split_axis=1, concat_axis=1, tiled=True)  51.5 us
    all_gather x1, waiting for transfers between devices, per_device(): whole = lax.all_gather(embeddings, 'trk', axis=2, tiled=True)  30.7 us
    all_to_all x1, blocking collectives, _extend_rates(): lax.all_to_all(jnp.stack([t0 for _ in range(lax.axis_size('seq'))]), 'seq...  26.6 us
    all_to_all x1, starting transfers between devices, per_device(): lax.all_to_all(blocks, 'seq', split_axis=1, concat_axis=1, tiled=True)  13.6 us
  transfers between devices with their start and end apart: 3, of which 3 were waited for; matrix products, arithmetic and copies ran while one was open for 1% of the time, Pallas kernels for 0%

profile of v1, /device:TPU:2, one launch (start us, length us, event | category | flops | bytes accessed | tf_op | source)
XLA Modules:
  0.0 614.8 jit_solution(17201438990222543362)
XLA Ops:
  7.2 0.0 all-gather.2.cloned.1.call-start
  7.2 0.7 all-gather.2.cloned.1.call-update
  7.9 0.8 copy.26
  8.8 0.7 add.46
  9.5 0.1 copy.27
  9.7 1.0 convert_reduce_fusion.2
  10.7 0.7 multiply_add_fusion
  11.4 1.4 convert_reduce_fusion
  12.8 0.4 convolution_convert_fusion
  13.2 30.7 %all-gather.2.cloned.1.call-done = bf16[4,128,1920]{1,2,0:T(8,128)(2,1)} async-done(((bf16[4,128,240]{1,2,0:T(8,128)(2,1)}), bf16[4,128,1920]{1,2,0:T(8,128)(2,1)}) %all-gather.2.cloned.1.call-update) | async-done | bytes 1966096 | tf_op jit(solution)/shard_map/all_gather | solution.py:44
  43.9 2.8 fusion.13
  46.8 2.2 fusion.9
  48.9 2.9 reshape.43
  51.8 3.5 copy.28
  55.4 13.6 %all-to-all-start = ((f32[4,64,4,512]{3,2,0,1:T(4,128)}), f32[4,64,4,512]{3,2,0,1:T(4,128)}, u32[]{:S(2)}, u32[]{:S(2)}) async-start(f32[4,64,4,512]{3,2,0,1:T(4,128)} %copy.28), calls=%async_computation | async-start | bytes 4194304 | tf_op jit(solution)/shard_map/all_to_all | solution.py:60
  68.9 0.0 all-reduce.4.cloned.1.call-start
  69.0 0.1 convert_reduce_fusion.1
  69.1 0.1 broadcast_compare_fusion
  69.2 51.5 %all-to-all-done = f32[4,64,4,512]{3,2,0,1:T(4,128)} async-done(((f32[4,64,4,512]{3,2,0,1:T(4,128)}), f32[4,64,4,512]{3,2,0,1:T(4,128)}, u32[]{:S(2)}, u32[]{:S(2)}) %all-to-all-start) | async-done | bytes 2097184 | tf_op jit(solution)/shard_map/all_to_all | solution.py:60
  120.7 2.1 fusion.20
  122.8 0.1 multiply_reduce_fusion
  122.9 284.7 %all-reduce.1 = (f32[4,512]{1,0:T(4,128)S(1)}, f32[4,512]{1,0:T(4,128)S(1)}, f32[4,512]{1,0:T(4,128)S(1)}) all-reduce(f32[4,512]{1,0:T(4,128)S(1)} %get-tuple-element.18, f32[4,512]{1,0:T(4,128)S(1)} %get-tuple-element.15, f32[4,512]{1,0:T(4,128)S(1)} %get-tuple-element.17), channel_id=1, replica_groups=mesh['seq'=64,'trk'=8] {'seq'}, use_global_device_ids=true, to_apply=%region_7.8 | all-reduce | flops 6144 | bytes 49152 | tf_op jit(solution)/shard_map/psum | solution.py:63
  407.6 0.6 fusion.16
  408.2 0.1 multiply_convert_fusion
  408.3 0.5 stack.2
  408.8 26.6 %all_to_all.10 = bf16[64,4,4,512]{3,1,2,0:T(4,128)(2,1)} all-to-all(bf16[64,4,4,512]{3,1,2,0:T(4,128)(2,1)S(1)} %stack.2), channel_id=1, replica_groups=mesh['seq'=64,'trk'=8] {'seq'}, dimensions={0} | all-to-all | bytes 2097152 | tf_op jit(solution)/shard_map/all_to_all | solution.py:10
  435.5 5.5 convolution_bitcast_fusion
  441.0 0.0 all-reduce.4.cloned.1.call-update
  441.0 1.3 dynamic-slice
  442.9 163.1 %all-reduce.4.cloned.1.call-done = f32[1920,512]{0,1:T(8,128)} async-done(((f32[1920,512]{0,1:T(8,128)}), f32[1920,512]{0,1:T(8,128)}) %all-reduce.4.cloned.1.call-update) | async-done | bytes 3932176
  606.0 1.2 constant_dynamic-slice_fusion
  607.2 0.8 copy.33
  (9 shorter events, 0.1 us)
Async XLA Ops:
  7.2 36.7 %copy-start = (bf16[1920,512]{1,0:T(8,128)(2,1)S(1)}, bf16[1920,512]{1,0:T(8,128)(2,1)}, u32[]{:S(2)}) copy-start(bf16[1920,512]{1,0:T(8,128)(2,1)} %param.7) | copy-start | bytes 5898244
  7.2 36.7 %all-gather.2.cloned.1.call-start = ((), (), s32[]{:S(2)}) async-start(), calls=%async_computation.2 | async-start | bytes 2211840 | tf_op jit(solution)/shard_map/all_gather | solution.py:44
  55.4 65.3 %all-to-all-start = ((f32[4,64,4,512]{3,2,0,1:T(4,128)}), f32[4,64,4,512]{3,2,0,1:T(4,128)}, u32[]{:S(2)}, u32[]{:S(2)}) async-start(f32[4,64,4,512]{3,2,0,1:T(4,128)} %copy.28), calls=%async_computation | async-start | bytes 4194304 | tf_op jit(solution)/shard_map/all_to_all | solution.py:60
  68.9 53.8 %copy-start.2 = (f32[4,4,512]{2,1,0:T(4,128)S(1)}, f32[4,4,512]{2,1,0:T(4,128)}, u32[]{:S(2)}) copy-start(f32[4,4,512]{2,1,0:T(4,128)} %param.11) | copy-start | bytes 98308
  68.9 537.1 %all-reduce.4.cloned.1.call-start = ((), (), s32[]{:S(2)}) async-start(), calls=%async_computation.3 | async-start | bytes 7864320
  122.7 318.2 %copy-start.1 = (f32[4,4,512]{2,1,0:T(4,128)}, f32[4,4,512]{2,1,0:T(4,128)S(1)}, u32[]{:S(2)}) copy-start(f32[4,4,512]{2,1,0:T(4,128)S(1)} %get-tuple-element.16) | copy-start | bytes 98308
Sparse Core Ops, SparseCore 0:
  10.1 33.7 all-gather.1
  441.1 164.8 all-reduce.3
